TPU v7x, 512 devices: a whole 4x8x8 slice. The times are simulated.
512 devices in a mesh: centre: 16 (over y, core), sample: 32 (over z, x).
Axes of the slice: x: 4, y: 8, z: 8, core: 2. Of those that a mesh axis runs over, the one named last changes fastest.
Arguments:
- centres: bfloat16 [1024, 32768], P(None, 'centre'), may hold values from -40 to 40
- pool: bfloat16 [1024, 32768], P('centre', 'sample'), may hold values from -40 to 40
- labels: int32 [32768], P('sample'), may hold values from 0 to 143
- picks: int32 [2, 16384], P(None, 'sample'), may hold values from 0 to 32767, as said below
- coefs: float32 [144, 32768], P(None, ('centre', 'sample')), may hold values from -192 to 1024000
Outputs:
- new_coefs: float32 [144, 32768], P(None, ('centre', 'sample'))
Inputs may be any that keep to these rules, and one draw needn't show every extreme that they name: `picks`: entry b of a step's batch is a pool column in [(b // 512) * 1024, (b // 512 + 1) * 1024); entries may repeat.
All inputs are finite; a program needn't handle non-finite values.
Results may differ from a plain program's by a relative error of at most 0.00065.
Values may be sent and summed in bfloat16 or wider, within the bound.
No kernel may reach another device: no remote copies, remote signals or barrier semaphores. Data moves between devices by JAX's collectives and lax.ppermute only.
A program may use at most 64 MiB of HBM per device.

v0:
```python
import jax
import jax.numpy as jnp
from jax import lax
from jax.sharding import PartitionSpec as P

STEPS = 2
LOGIT_GAIN = 16.0
LENGTH_SCALE = 0.5
STEP_GAIN = 2048.0
EPS = 1e-06


def from_everyone(array, axis):
    peers = lax.axis_size(axis)
    return lax.all_to_all(
        jnp.broadcast_to(array[None], (peers, *array.shape)), axis, 0, 0, tiled=True
    )


def joined_along(parts, dim):
    dims = list(parts.shape[1:])
    dims[dim] *= parts.shape[0]
    return jnp.moveaxis(parts, 0, dim).reshape(dims)


def collect(array, axis, dim):
    parts = from_everyone(array, axis)
    return joined_along(parts, dim)


def over_pieces(array, axis):
    return lax.all_gather(array, axis).sum(0)


def cut_along(array, dim, peers):
    dims = array.shape
    parts = array.reshape(*dims[:dim], peers, dims[dim] // peers, *dims[dim + 1 :])
    return jnp.moveaxis(parts, dim, 0)


def summed_on_arrival(array, axis, dim):
    peers = lax.axis_size(axis)
    parts = lax.all_to_all(cut_along(array, dim, peers), axis, 0, 0, tiled=True)
    return jnp.sum(parts, axis=0)


def laplace(cross, sample_sq, centre_sq, width):
    mean_sq = (sample_sq[:, None] + centre_sq[None, :] - 2.0 * cross) / width
    return jnp.exp(-jnp.sqrt(mean_sq + EPS) / LENGTH_SCALE).astype(jnp.bfloat16)


def on_device(centres, pool, labels, picks, coefs):
    width = centres.shape[0]
    cen_dev = centres.shape[1]
    pool_dev = pool.shape[1]
    batch_dev = picks.shape[1]
    classes = coefs.shape[0]
    total_centres = cen_dev * lax.axis_size("centre")
    total_batch = batch_dev * lax.axis_size("sample")
    rate = STEP_GAIN * LOGIT_GAIN / total_batch
    centre_sq = jnp.sum(jnp.square(centres.astype(jnp.float32)), axis=0)
    local_picks = picks - lax.axis_index("sample") * pool_dev
    current = coefs
    for step in range(STEPS):
        coef_half = collect(current.astype(jnp.bfloat16), "sample", 1)
        chosen = local_picks[step]
        feats = jnp.take(pool, chosen, axis=1)
        labs = jnp.take(labels, chosen)
        gathered = lax.all_gather(feats, "centre", axis=0, tiled=True)
        cross = lax.dot_general(
            gathered, centres, (((0,), (0,)), ((), ())), preferred_element_type=jnp.float32
        )
        sample_sq = jnp.sum(jnp.square(gathered.astype(jnp.float32)), axis=0)
        kern = laplace(cross, sample_sq, centre_sq, width)
        partial_logits = lax.dot_general(
            coef_half, kern, (((1,), (1,)), ((), ())), preferred_element_type=jnp.float32
        )
        logits = over_pieces(partial_logits, "centre") * (LOGIT_GAIN / total_centres)
        top = jnp.max(logits, axis=0, keepdims=True)
        expo = jnp.exp(logits - top)
        probs = expo / jnp.sum(expo, axis=0, keepdims=True)
        class_ids = jnp.arange(classes, dtype=jnp.int32)
        onehot = (class_ids[:, None] == labs[None, :]).astype(jnp.float32)
        resid = (probs - onehot).astype(jnp.bfloat16)
        grad_part = jnp.dot(resid, kern, preferred_element_type=jnp.float32)
        current = current - rate * summed_on_arrival(grad_part, "sample", 1)
    return current


def solution(mesh):
    placed = (
        P(None, "centre"),
        P("centre", "sample"),
        P("sample"),
        P(None, "sample"),
        P(None, ("centre", "sample")),
    )
    return jax.shard_map(
        on_device,
        mesh=mesh,
        in_specs=placed,
        out_specs=P(None, ("centre", "sample")),
        check_vma=False,
    )
```

profile of v0, /device:TPU:2, one launch (start us, length us, event | category | flops | bytes accessed | tf_op | source)
XLA Modules:
  0.0 336.5 jit_solution(12417494301291164431)
XLA Ops:
  6.5 0.0 copy-start
  6.5 0.0 all-gather.7.cloned.1.call-start
  6.5 0.7 broadcast_subtract_fusion
  7.3 0.0 copy-done
  7.3 2.3 gather_fusion.1
  9.6 1.1 copy.40
  10.7 1.3 gather_fusion
  12.0 0.1 select_bitcast_fusion.1
  12.2 0.7 copy.41
  12.9 0.0 all-gather.7.cloned.1.call-update
  12.9 0.8 convert_element_type.36
  13.8 1.2 broadcast_in_dim.19
  14.9 13.5 %all-to-all-start = ((bf16[32,144,64]{1,2,0:T(8,128)(2,1)}), bf16[32,144,64]{1,2,0:T(8,128)(2,1)S(1)}, u32[]{:S(2)}, u32[]{:S(2)}) async-start(bf16[32,144,64]{1,2,0:T(8,128)(2,1)} %broadcast_in_dim.19), calls=%async_computation | async-start | bytes 2097152 | tf_op jit(solution)/shard_map/all_to_all | solution.py:15
  28.4 0.0 all-gather.11.cloned.1.call-start
  28.4 3.1 multiply_reduce_fusion
  31.5 27.1 %all-gather.7.cloned.1.call-done = bf16[1024,512]{1,0:T(8,128)(2,1)} async-done(((bf16[64,512]{1,0:T(8,128)(2,1)}), bf16[1024,512]{1,0:T(8,128)(2,1)}) %all-gather.7.cloned.1.call-update) | async-done | bytes 1048592 | tf_op jit(solution)/shard_map/all_gather | solution.py:69
  58.6 1.5 multiply_reduce_fusion.2
  60.1 6.8 %exponential_convert_fusion.1 = bf16[512,2048]{1,0:T(8,128)(2,1)S(1)} fusion(bf16[1024,512]{1,0:T(8,128)(2,1)} %all-gather.7.cloned.1.call-done, bf16[1024,2048]{1,0:T(8,128)(2,1)} %param.9, f32[2048]{0:T(1024)S(1)} %multiply_reduce_fusion, f32[512]{0:T(512)S(1)} %multiply_reduce_fusion.2), kind=kOutput, calls=%fused_computation.6 | convolution fusion | flops 2155872256 | bytes 7350272 | tf_op jit(solution)/shard_map/dot_general | solution.py:70
  66.8 0.0 all-to-all-done
  66.9 1.6 convolution_bitcast_fusion
  68.4 0.0 all-gather.11.cloned.1.call-update
  68.4 44.5 %all-gather.11.cloned.1.call-done = f32[2304,512]{1,0:T(8,128)} async-done(((f32[144,512]{1,0:T(8,128)}), f32[2304,512]{1,0:T(8,128)}) %all-gather.11.cloned.1.call-update) | async-done | bytes 4718608 | tf_op jit(solution)/shard_map/all_gather | solution.py:32
  113.0 2.9 reduce_sum.83
  115.9 0.1 fusion
  116.0 1.6 fusion.2
  117.5 2.1 reshape.34
  119.6 2.4 copy.43
  122.0 0.0 copy-start.4
  122.0 10.6 %all-to-all-start.1 = ((f32[32,144,64]{1,2,0:T(8,128)}), f32[32,144,64]{1,2,0:T(8,128)S(1)}, u32[]{:S(2)}, u32[]{:S(2)}) async-start(f32[32,144,64]{1,2,0:T(8,128)} %copy.43), calls=%async_computation.1 | async-start | bytes 4194304 | tf_op jit(solution)/shard_map/all_to_all | solution.py:43
  132.7 0.0 all-gather.9.cloned.1.call-start
  132.7 2.3 gather_fusion.3
  135.0 1.3 gather_fusion.2
  136.4 0.1 select_bitcast_fusion
  136.6 0.7 copy.48
  137.3 0.0 all-gather.9.cloned.1.call-update
  137.3 45.0 %all-to-all-done.1 = f32[32,144,64]{1,2,0:T(8,128)S(1)} async-done(((f32[32,144,64]{1,2,0:T(8,128)}), f32[32,144,64]{1,2,0:T(8,128)S(1)}, u32[]{:S(2)}, u32[]{:S(2)}) %all-to-all-start.1) | async-done | bytes 1179680 | tf_op jit(solution)/shard_map/all_to_all | solution.py:43
  182.3 0.1 reduce_sum.85
  182.5 0.0 copy-done.4
  182.5 0.0 copy-start.2
  182.5 1.1 broadcast_in_dim.20
  183.6 6.5 %all-to-all-start.2 = ((bf16[32,144,64]{1,2,0:T(8,128)(2,1)}), bf16[32,144,64]{1,2,0:T(8,128)(2,1)S(1)}, u32[]{:S(2)}, u32[]{:S(2)}) async-start(bf16[32,144,64]{1,2,0:T(8,128)(2,1)} %broadcast_in_dim.20), calls=%async_computation.2 | async-start | bytes 2097152 | tf_op jit(solution)/shard_map/all_to_all | solution.py:15
  190.1 0.0 all-gather.13.cloned.1.call-start
  190.1 0.0 all-gather.9.cloned.1.call-done
  190.2 0.0 copy-done.2
  190.2 1.5 multiply_reduce_fusion.1
  191.7 6.7 %exponential_convert_fusion = bf16[512,2048]{1,0:T(8,128)(2,1)S(1)} fusion(bf16[1024,512]{1,0:T(8,128)(2,1)} %all-gather.9.cloned.1.call-done, bf16[1024,2048]{1,0:T(8,128)(2,1)} %param.9, f32[512]{0:T(512)S(1)} %multiply_reduce_fusion.1, f32[2048]{0:T(1024)S(1)} %multiply_reduce_fusion), kind=kOutput, calls=%fused_computation.5 | convolution fusion | flops 2155872256 | bytes 7350272 | tf_op jit(solution)/shard_map/dot_general | solution.py:70
  198.4 0.0 copy-start.1
  198.4 19.8 %all-to-all-done.2 = bf16[32,144,64]{1,2,0:T(8,128)(2,1)S(1)} async-done(((bf16[32,144,64]{1,2,0:T(8,128)(2,1)}), bf16[32,144,64]{1,2,0:T(8,128)(2,1)S(1)}, u32[]{:S(2)}, u32[]{:S(2)}) %all-to-all-start.2) | async-done | bytes 589856 | tf_op jit(solution)/shard_map/all_to_all | solution.py:15
  218.2 1.6 fusion.16
  219.8 0.0 all-gather.13.cloned.1.call-update
  219.8 39.4 %all-gather.13.cloned.1.call-done = f32[2304,512]{1,0:T(8,128)} async-done(((f32[144,512]{1,0:T(8,128)}), f32[2304,512]{1,0:T(8,128)}) %all-gather.13.cloned.1.call-update) | async-done | bytes 4718608 | tf_op jit(solution)/shard_map/all_gather | solution.py:32
  259.2 0.0 copy-done.1
  259.2 2.9 reduce_sum.87
  262.1 0.1 fusion.1
  262.1 2.1 fusion.3
  264.3 0.9 reshape.36
  265.2 2.4 copy.49
  267.6 0.0 copy-start.3
  267.6 0.0 copy-start.5
  267.6 61.6 %all_to_all.20 = f32[32,144,64]{1,2,0:T(8,128)S(1)} all-to-all(f32[32,144,64]{1,2,0:T(8,128)} %copy.49), channel_id=1, replica_groups=mesh['centre'=16,'sample'=32] {'sample'}, dimensions={0} | all-to-all | bytes 2359296 | tf_op jit(solution)/shard_map/all_to_all | solution.py:43
  329.2 0.1 reduce_sum.89
  329.4 0.0 copy-done.3
  329.4 0.0 copy-done.5
  329.4 0.6 multiply_subtract_fusion
  (10 shorter events, 0.1 us)
Async XLA Ops:
  6.5 0.7 copy-start
  6.5 52.0 %all-gather.7.cloned.1.call-start = ((), (), s32[]{:S(2)}) async-start(), calls=%async_computation.4 | async-start | bytes 1114112 | tf_op jit(solution)/shard_map/all_gather | solution.py:69
  14.9 51.9 %all-to-all-start = ((bf16[32,144,64]{1,2,0:T(8,128)(2,1)}), bf16[32,144,64]{1,2,0:T(8,128)(2,1)S(1)}, u32[]{:S(2)}, u32[]{:S(2)}) async-start(bf16[32,144,64]{1,2,0:T(8,128)(2,1)} %broadcast_in_dim.19), calls=%async_computation | async-start | bytes 2097152 | tf_op jit(solution)/shard_map/all_to_all | solution.py:15
  28.4 84.6 %all-gather.11.cloned.1.call-start = ((), (), s32[]{:S(2)}) async-start(), calls=%async_computation.6 | async-start | bytes 5013504 | tf_op jit(solution)/shard_map/all_gather | solution.py:32
  122.0 60.4 %copy-start.4 = (f32[144,64]{0,1:T(8,128)S(1)}, f32[144,64]{0,1:T(8,128)}, u32[]{:S(2)}) copy-start(f32[144,64]{0,1:T(8,128)} %param.13) | copy-start | bytes 110596
  122.0 60.3 %all-to-all-start.1 = ((f32[32,144,64]{1,2,0:T(8,128)}), f32[32,144,64]{1,2,0:T(8,128)S(1)}, u32[]{:S(2)}, u32[]{:S(2)}) async-start(f32[32,144,64]{1,2,0:T(8,128)} %copy.43), calls=%async_computation.1 | async-start | bytes 4194304 | tf_op jit(solution)/shard_map/all_to_all | solution.py:43
  132.7 57.5 %all-gather.9.cloned.1.call-start = ((), (), s32[]{:S(2)}) async-start(), calls=%async_computation.5 | async-start | bytes 1114112 | tf_op jit(solution)/shard_map/all_gather | solution.py:69
  182.5 7.7 %copy-start.2 = (f32[144,64]{0,1:T(8,128)}, f32[144,64]{0,1:T(8,128)S(1)}, u32[]{:S(2)}) copy-start(f32[144,64]{0,1:T(8,128)S(1)} %reduce_sum.85) | copy-start | bytes 110596
  183.6 34.6 %all-to-all-start.2 = ((bf16[32,144,64]{1,2,0:T(8,128)(2,1)}), bf16[32,144,64]{1,2,0:T(8,128)(2,1)S(1)}, u32[]{:S(2)}, u32[]{:S(2)}) async-start(bf16[32,144,64]{1,2,0:T(8,128)(2,1)} %broadcast_in_dim.20), calls=%async_computation.2 | async-start | bytes 2097152 | tf_op jit(solution)/shard_map/all_to_all | solution.py:15
  190.1 69.1 %all-gather.13.cloned.1.call-start = ((), (), s32[]{:S(2)}) async-start(), calls=%async_computation.7 | async-start | bytes 5013504 | tf_op jit(solution)/shard_map/all_gather | solution.py:32
  198.4 60.7 %copy-start.1 = (bf16[512,2048]{1,0:T(8,128)(2,1)}, bf16[512,2048]{1,0:T(8,128)(2,1)S(1)}, u32[]{:S(2)}) copy-start(bf16[512,2048]{1,0:T(8,128)(2,1)S(1)} %exponential_convert_fusion) | copy-start | bytes 6291460
  267.6 61.7 %copy-start.3 = (f32[144,64]{0,1:T(8,128)S(1)}, f32[144,64]{0,1:T(8,128)}, u32[]{:S(2)}) copy-start(f32[144,64]{0,1:T(8,128)} %copy-done.2) | copy-start | bytes 110596
  267.6 61.7 %copy-start.5 = (f32[144,64]{0,1:T(8,128)S(1)}, f32[144,64]{0,1:T(8,128)}, u32[]{:S(2)}) copy-start(f32[144,64]{0,1:T(8,128)} %param.13) | copy-start | bytes 110596
Sparse Core Ops, SparseCore 0:
  13.0 45.5 all-gather.6
  68.6 44.3 all-gather.10
  137.4 38.9 all-gather.8
  219.9 39.2 all-gather.12
where the time goes:
time: 337 us
  waiting for transfers between devices  176 us (52%)
  blocking collectives  61.6 us (18%)
  starting transfers between devices  30.7 us (9%)
  matrix products  20.3 us (6%)
  local copies, waits for them, and re-layouts  19.9 us (6%)
  other arithmetic  14.8 us (4%)
  between operations  13.4 us (4%)
    all_gather x2, waiting for transfers between devices, over_pieces(): return lax.all_gather(array, axis).sum(0)  83.9 us
    all_to_all x1, blocking collectives, summed_on_arrival(): parts = lax.all_to_all(cut_along(array, dim, peers), axis, 0, 0, tiled=True)  61.6 us
    all_to_all x1, waiting for transfers between devices, summed_on_arrival(): parts = lax.all_to_all(cut_along(array, dim, peers), axis, 0, 0, tiled=True)  45 us
    all_gather x2, waiting for transfers between devices, on_device(): gathered = lax.all_gather(feats, 'centre', axis=0, tiled=True)  27.1 us
    all_to_all x2, starting transfers between devices, from_everyone(): lax.all_to_all(jnp.broadcast_to(array[None], (peers, *array.shape)), axis...  19.9 us
    all_to_all x2, waiting for transfers between devices, from_everyone(): lax.all_to_all(jnp.broadcast_to(array[None], (peers, *array.shape)), axis...  19.8 us
    dot_general x2, matrix products, on_device(): lax.dot_general(gathered, centres, (((0,), (0,)), ((), ())), preferred_el...  13.5 us
    all_to_all x1, starting transfers between devices, summed_on_arrival(): parts = lax.all_to_all(cut_along(array, dim, peers), axis, 0, 0, tiled=True)  10.6 us
  transfers between devices with their start and end apart: 7, of which 5 were waited for; matrix products, arithmetic and copies ran while one was open for 8% of the time, Pallas kernels for 0%

commit v1 on v0

--- a/solution.py
+++ b/solution.py
@@ -66,7 +66,16 @@
         chosen = local_picks[step]
         feats = jnp.take(pool, chosen, axis=1)
         labs = jnp.take(labels, chosen)
-        gathered = lax.all_gather(feats, "centre", axis=0, tiled=True)
+        ways = lax.axis_size("centre")
+        up = [(d, (d + 1) % ways) for d in range(ways)]
+        down = [(d, (d - 1) % ways) for d in range(ways)]
+        earlier, later = ([feats], [feats])
+        for _ in range(ways // 2):
+            earlier.append(lax.ppermute(earlier[-1], "centre", up))
+        for _ in range((ways - 1) // 2):
+            later.append(lax.ppermute(later[-1], "centre", down))
+        line = jnp.concatenate([*earlier[::-1], *later[1:]], axis=0)
+        gathered = jnp.roll(line, (lax.axis_index("centre") - ways // 2) * feats.shape[0], axis=0)
         cross = lax.dot_general(
             gathered, centres, (((0,), (0,)), ((), ())), preferred_element_type=jnp.float32
         )

time: 337 us -> 367 us (1.089)
  starting transfers between devices: 30.7 us -> 71.5 us
  waiting for transfers between devices: 176 us -> 163 us
    ppermute x0 -> x30, starting transfers between devices: none -> 41 us  [the longest x14 41 us: on_device(): later.append(lax.ppermute(later[-1], 'centre', down))]
    ppermute x0 -> x30, waiting for transfers between devices: none -> 38.8 us  [the longest x16 28.5 us: on_device(): earlier.append(lax.ppermute(earlier[-1], 'centre', up))]
    all_gather x2 -> x0, waiting for transfers between devices: 27.1 us -> none  [on_device(): gathered = lax.all_gather(feats, 'centre', axis=0, tiled=True)]
    all_to_all x1, waiting for transfers between devices: 45 us -> 29 us  [summed_on_arrival(): parts = lax.all_to_all(cut_along(array, dim, peers), axis, 0, 0, tiled=True)]
    all_to_all x2, waiting for transfers between devices: 19.8 us -> 7.3 us  [from_everyone(): lax.all_to_all(jnp.broadcast_to(array[None], (peers, *array.shape)), axis...]
    all_gather x2, waiting for transfers between devices: 83.9 us -> 88 us  [over_pieces(): return lax.all_gather(array, axis).sum(0)]
  transfers between devices with their start and end apart: 7 -> 35, of which waited for: 5 -> 20; matrix products, arithmetic and copies ran while one was open for 8% -> 7% of each run, Pallas kernels for 0% -> 0%
where the time goes in v1:
time: 367 us; the launch traced here: 366 us
  waiting for transfers between devices  163 us (44%)
  starting transfers between devices  71.5 us (19%)
  blocking collectives  61.5 us (17%)
  matrix products  22.9 us (6%)
  local copies, waits for them, and re-layouts  20.1 us (5%)
  between operations  13.7 us (4%)
  other arithmetic  13.5 us (4%)
    all_gather x2, waiting for transfers between devices, over_pieces(): return lax.all_gather(array, axis).sum(0)  88 us
    all_to_all x1, blocking collectives, summed_on_arrival(): parts = lax.all_to_all(cut_along(array, dim, peers), axis, 0, 0, tiled=True)  61.5 us
    ppermute x14, starting transfers between devices, on_device(): later.append(lax.ppermute(later[-1], 'centre', down))  41 us
    all_to_all x1, waiting for transfers between devices, summed_on_arrival(): parts = lax.all_to_all(cut_along(array, dim, peers), axis, 0, 0, tiled=True)  29 us
    ppermute x16, waiting for transfers between devices, on_device(): earlier.append(lax.ppermute(earlier[-1], 'centre', up))  28.5 us
    all_to_all x2, starting transfers between devices, from_everyone(): lax.all_to_all(jnp.broadcast_to(array[None], (peers, *array.shape)), axis...  19.9 us
    dot_general x2, matrix products, on_device(): lax.dot_general(gathered, centres, (((0,), (0,)), ((), ())), preferred_el...  12.8 us
    all_to_all x1, starting transfers between devices, summed_on_arrival(): parts = lax.all_to_all(cut_along(array, dim, peers), axis, 0, 0, tiled=True)  10.5 us
  transfers between devices with their start and end apart: 35, of which 20 were waited for; matrix products, arithmetic and copies ran while one was open for 7% of the time, Pallas kernels for 0%

profile of v1, /device:TPU:2, one launch (start us, length us, event | category | flops | bytes accessed | tf_op | source)
XLA Modules:
  0.0 366.3 jit_solution(12091705410267244209)
XLA Ops:
  6.5 0.7 broadcast_subtract_fusion
  7.3 2.3 gather_fusion.1
  9.6 0.2 copy.36
  9.8 1.3 gather_fusion
  11.3 2.9 collective-permute-start.8
  14.3 2.6 collective-permute-done
  16.9 3.0 collective-permute-start.9
  19.9 2.6 collective-permute-done.1
  22.5 3.0 collective-permute-start.10
  25.5 2.6 collective-permute-done.2
  28.1 3.0 collective-permute-start.11
  31.1 2.6 collective-permute-done.3
  33.7 3.0 collective-permute-start.12
  36.7 2.6 collective-permute-done.4
  39.3 3.0 collective-permute-start.13
  42.3 2.6 collective-permute-done.5
  44.9 1.1 broadcast_in_dim.19
  46.1 13.5 %all-to-all-start = ((bf16[32,144,64]{1,2,0:T(8,128)(2,1)}), bf16[32,144,64]{1,2,0:T(8,128)(2,1)}, u32[]{:S(2)}, u32[]{:S(2)}) async-start(bf16[32,144,64]{1,2,0:T(8,128)(2,1)} %broadcast_in_dim.19), calls=%async_computation | async-start | bytes 2097152 | tf_op jit(solution)/shard_map/all_to_all | solution.py:15
  59.6 2.4 collective-permute-start.14
  62.0 3.1 multiply_reduce_fusion
  65.1 2.5 collective-permute-done.7
  67.6 1.0 concatenate.9
  68.6 1.2 multiply_reduce_fusion.2
  69.9 6.4 %exponential_convert_fusion.1 = bf16[512,2048]{1,0:T(8,128)(2,1)S(1)} fusion(bf16[1024,2048]{1,0:T(8,128)(2,1)} %param.11, f32[2048]{0:T(1024)S(1)} %multiply_reduce_fusion, f32[512]{0:T(512)S(1)} %multiply_reduce_fusion.2, s32[]{:T(128)S(6)} %select_n.34, bf16[1024,512]{0,1:T(8,128)(2,1)S(1)} %concatenate.9), kind=kOutput, calls=%fused_computation.6 | convolution fusion | flops 2157969408 | bytes 7350276 | tf_op jit(solution)/shard_map/dot_general | solution.py:79
  76.3 7.3 %all-to-all-done = bf16[32,144,64]{1,2,0:T(8,128)(2,1)} async-done(((bf16[32,144,64]{1,2,0:T(8,128)(2,1)}), bf16[32,144,64]{1,2,0:T(8,128)(2,1)}, u32[]{:S(2)}, u32[]{:S(2)}) %all-to-all-start) | async-done | bytes 589856 | tf_op jit(solution)/shard_map/all_to_all | solution.py:15
  83.6 2.8 convolution_bitcast_fusion
  86.4 44.3 %all-gather.5.cloned.1.call-done = f32[2304,512]{1,0:T(8,128)} async-done(((f32[144,512]{1,0:T(8,128)}), f32[2304,512]{1,0:T(8,128)}) %all-gather.5.cloned.1.call-update) | async-done | bytes 4718608 | tf_op jit(solution)/shard_map/all_gather | solution.py:32
  130.7 2.9 reduce_sum.83
  133.7 1.6 fusion.4
  135.3 2.1 reshape.34
  137.4 2.4 copy.38
  139.7 10.5 %all-to-all-start.1 = ((f32[32,144,64]{1,2,0:T(8,128)}), f32[32,144,64]{1,2,0:T(8,128)S(1)}, u32[]{:S(2)}, u32[]{:S(2)}) async-start(f32[32,144,64]{1,2,0:T(8,128)} %copy.38), calls=%async_computation.1 | async-start | bytes 4194304 | tf_op jit(solution)/shard_map/all_to_all | solution.py:43
  150.3 2.3 gather_fusion.3
  152.6 1.3 gather_fusion.2
  154.1 2.9 collective-permute-start.23
  157.1 2.6 collective-permute-done.15
  159.7 3.2 collective-permute-start.24
  163.0 2.4 collective-permute-done.16
  165.5 3.4 collective-permute-start.25
  168.9 2.1 collective-permute-done.17
  170.9 29.0 %all-to-all-done.1 = f32[32,144,64]{1,2,0:T(8,128)S(1)} async-done(((f32[32,144,64]{1,2,0:T(8,128)}), f32[32,144,64]{1,2,0:T(8,128)S(1)}, u32[]{:S(2)}, u32[]{:S(2)}) %all-to-all-start.1) | async-done | bytes 1179680 | tf_op jit(solution)/shard_map/all_to_all | solution.py:43
  200.1 1.1 broadcast_in_dim.20
  201.2 6.4 %all-to-all-start.2 = ((bf16[32,144,64]{1,2,0:T(8,128)(2,1)}), bf16[32,144,64]{1,2,0:T(8,128)(2,1)}, u32[]{:S(2)}, u32[]{:S(2)}) async-start(bf16[32,144,64]{1,2,0:T(8,128)(2,1)} %broadcast_in_dim.20), calls=%async_computation.2 | async-start | bytes 2097152 | tf_op jit(solution)/shard_map/all_to_all | solution.py:15
  207.6 1.0 collective-permute-start.26
  208.6 2.5 collective-permute-done.26
  211.1 3.3 collective-permute-start.27
  214.4 2.5 collective-permute-done.27
  217.0 3.5 collective-permute-start.28
  220.4 2.5 collective-permute-done.28
  223.0 3.5 collective-permute-start.29
  226.4 2.5 collective-permute-done.29
  229.0 3.1 collective-permute-done.22
  232.0 1.0 concatenate.10
  233.0 1.2 multiply_reduce_fusion.1
  234.3 6.4 %exponential_convert_fusion = bf16[512,2048]{1,0:T(8,128)(2,1)S(1)} fusion(bf16[1024,2048]{1,0:T(8,128)(2,1)} %param.11, f32[512]{0:T(512)S(1)} %multiply_reduce_fusion.1, f32[2048]{0:T(1024)S(1)} %multiply_reduce_fusion, s32[]{:T(128)S(6)} %select_n.34, bf16[1024,512]{0,1:T(8,128)(2,1)S(1)} %concatenate.10), kind=kOutput, calls=%fused_computation.5 | convolution fusion | flops 2157969408 | bytes 7350276 | tf_op jit(solution)/shard_map/dot_general | solution.py:79
  240.7 3.6 fusion.20
  244.3 43.7 %all-gather.7.cloned.1.call-done = f32[2304,512]{1,0:T(8,128)} async-done(((f32[144,512]{1,0:T(8,128)}), f32[2304,512]{1,0:T(8,128)}) %all-gather.7.cloned.1.call-update) | async-done | bytes 4718608 | tf_op jit(solution)/shard_map/all_gather | solution.py:32
  288.1 2.9 reduce_sum.87
  291.1 2.1 fusion.5
  293.2 0.9 reshape.36
  294.1 2.4 copy.43
  296.5 61.5 %all_to_all.20 = f32[32,144,64]{1,2,0:T(8,128)S(1)} all-to-all(f32[32,144,64]{1,2,0:T(8,128)} %copy.43), channel_id=1, replica_groups=mesh['centre'=16,'sample'=32] {'sample'}, dimensions={0} | all-to-all | bytes 2359296 | tf_op jit(solution)/shard_map/all_to_all | solution.py:43
  358.1 0.7 copy-done.3
  358.8 0.6 multiply_subtract_fusion
  (66 shorter events, 1.3 us)
Async XLA Ops:
  6.5 0.8 copy-start
  6.5 3.1 copy-start.6
  6.5 38.4 %copy-start.4 = (f32[144,64]{0,1:T(8,128)S(1)}, f32[144,64]{0,1:T(8,128)}, u32[]{:S(2)}) copy-start(f32[144,64]{0,1:T(8,128)} %param.15) | copy-start | bytes 110596
  11.3 5.6 %collective-permute-start = (bf16[64,512]{0,1:T(8,128)(2,1)S(1)}, bf16[64,512]{0,1:T(8,128)(2,1)S(1)}, u32[]{:S(2)}, u32[]{:S(2)}) collective-permute-start(bf16[64,512]{0,1:T(8,128)(2,1)S(1)} %select_bitcast_fusion.1), channel_id=1, source_target_pairs={{0,32},{32,64},{64,96},{96,128},{128,160},{160,192},{192,224},{224... | collective-permute-start | bytes 196616 | tf_op jit(solution)/shard_map/ppermute | solution.py:74
  11.3 5.6 %collective-permute-start.8 = (bf16[64,512]{0,1:T(8,128)(2,1)S(1)}, bf16[64,512]{0,1:T(8,128)(2,1)S(1)}, u32[]{:S(2)}, u32[]{:S(2)}) collective-permute-start(bf16[64,512]{0,1:T(8,128)(2,1)S(1)} %select_bitcast_fusion.1), channel_id=1, source_target_pairs={{0,480},{32,0},{64,32},{96,64},{128,96},{160,128},{192,160},{224,1... | collective-permute-start | bytes 196616 | tf_op jit(solution)/shard_map/ppermute | solution.py:76
  16.9 5.6 %collective-permute-start.1 = (bf16[64,512]{0,1:T(8,128)(2,1)S(1)}, bf16[64,512]{0,1:T(8,128)(2,1)S(1)}, u32[]{:S(2)}, u32[]{:S(2)}) collective-permute-start(bf16[64,512]{0,1:T(8,128)(2,1)S(1)} %collective-permute-done), channel_id=1, source_target_pairs={{0,32},{32,64},{64,96},{96,128},{128,160},{160,192},{192,224},{224... | collective-permute-start | bytes 196616 | tf_op jit(solution)/shard_map/ppermute | solution.py:74
  16.9 5.6 %collective-permute-start.9 = (bf16[64,512]{0,1:T(8,128)(2,1)S(1)}, bf16[64,512]{0,1:T(8,128)(2,1)S(1)}, u32[]{:S(2)}, u32[]{:S(2)}) collective-permute-start(bf16[64,512]{0,1:T(8,128)(2,1)S(1)} %collective-permute-done.8), channel_id=1, source_target_pairs={{0,480},{32,0},{64,32},{96,64},{128,96},{160,128},{192,160},{224,1... | collective-permute-start | bytes 196616 | tf_op jit(solution)/shard_map/ppermute | solution.py:76
  22.5 5.6 %collective-permute-start.2 = (bf16[64,512]{0,1:T(8,128)(2,1)S(1)}, bf16[64,512]{0,1:T(8,128)(2,1)S(1)}, u32[]{:S(2)}, u32[]{:S(2)}) collective-permute-start(bf16[64,512]{0,1:T(8,128)(2,1)S(1)} %collective-permute-done.1), channel_id=1, source_target_pairs={{0,32},{32,64},{64,96},{96,128},{128,160},{160,192},{192,224},{224... | collective-permute-start | bytes 196616 | tf_op jit(solution)/shard_map/ppermute | solution.py:74
  22.5 5.6 %collective-permute-start.10 = (bf16[64,512]{0,1:T(8,128)(2,1)S(1)}, bf16[64,512]{0,1:T(8,128)(2,1)S(1)}, u32[]{:S(2)}, u32[]{:S(2)}) collective-permute-start(bf16[64,512]{0,1:T(8,128)(2,1)S(1)} %collective-permute-done.9), channel_id=1, source_target_pairs={{0,480},{32,0},{64,32},{96,64},{128,96},{160,128},{192,160},{224,1... | collective-permute-start | bytes 196616 | tf_op jit(solution)/shard_map/ppermute | solution.py:76
  28.1 5.6 %collective-permute-start.3 = (bf16[64,512]{0,1:T(8,128)(2,1)S(1)}, bf16[64,512]{0,1:T(8,128)(2,1)S(1)}, u32[]{:S(2)}, u32[]{:S(2)}) collective-permute-start(bf16[64,512]{0,1:T(8,128)(2,1)S(1)} %collective-permute-done.2), channel_id=1, source_target_pairs={{0,32},{32,64},{64,96},{96,128},{128,160},{160,192},{192,224},{224... | collective-permute-start | bytes 196616 | tf_op jit(solution)/shard_map/ppermute | solution.py:74
  28.1 5.6 %collective-permute-start.11 = (bf16[64,512]{0,1:T(8,128)(2,1)S(1)}, bf16[64,512]{0,1:T(8,128)(2,1)S(1)}, u32[]{:S(2)}, u32[]{:S(2)}) collective-permute-start(bf16[64,512]{0,1:T(8,128)(2,1)S(1)} %collective-permute-done.10), channel_id=1, source_target_pairs={{0,480},{32,0},{64,32},{96,64},{128,96},{160,128},{192,160},{224,1... | collective-permute-start | bytes 196616 | tf_op jit(solution)/shard_map/ppermute | solution.py:76
  33.7 5.6 %collective-permute-start.4 = (bf16[64,512]{0,1:T(8,128)(2,1)S(1)}, bf16[64,512]{0,1:T(8,128)(2,1)S(1)}, u32[]{:S(2)}, u32[]{:S(2)}) collective-permute-start(bf16[64,512]{0,1:T(8,128)(2,1)S(1)} %collective-permute-done.3), channel_id=1, source_target_pairs={{0,32},{32,64},{64,96},{96,128},{128,160},{160,192},{192,224},{224... | collective-permute-start | bytes 196616 | tf_op jit(solution)/shard_map/ppermute | solution.py:74
  33.7 5.6 %collective-permute-start.12 = (bf16[64,512]{0,1:T(8,128)(2,1)S(1)}, bf16[64,512]{0,1:T(8,128)(2,1)S(1)}, u32[]{:S(2)}, u32[]{:S(2)}) collective-permute-start(bf16[64,512]{0,1:T(8,128)(2,1)S(1)} %collective-permute-done.11), channel_id=1, source_target_pairs={{0,480},{32,0},{64,32},{96,64},{128,96},{160,128},{192,160},{224,1... | collective-permute-start | bytes 196616 | tf_op jit(solution)/shard_map/ppermute | solution.py:76
  39.3 5.6 %collective-permute-start.5 = (bf16[64,512]{0,1:T(8,128)(2,1)S(1)}, bf16[64,512]{0,1:T(8,128)(2,1)S(1)}, u32[]{:S(2)}, u32[]{:S(2)}) collective-permute-start(bf16[64,512]{0,1:T(8,128)(2,1)S(1)} %collective-permute-done.4), channel_id=1, source_target_pairs={{0,32},{32,64},{64,96},{96,128},{128,160},{160,192},{192,224},{224... | collective-permute-start | bytes 196616 | tf_op jit(solution)/shard_map/ppermute | solution.py:74
  39.3 20.3 %collective-permute-start.13 = (bf16[64,512]{0,1:T(8,128)(2,1)S(1)}, bf16[64,512]{0,1:T(8,128)(2,1)S(1)}, u32[]{:S(2)}, u32[]{:S(2)}) collective-permute-start(bf16[64,512]{0,1:T(8,128)(2,1)S(1)} %collective-permute-done.12), channel_id=1, source_target_pairs={{0,480},{32,0},{64,32},{96,64},{128,96},{160,128},{192,160},{224,1... | collective-permute-start | bytes 196616 | tf_op jit(solution)/shard_map/ppermute | solution.py:76
  44.9 17.1 %collective-permute-start.6 = (bf16[64,512]{0,1:T(8,128)(2,1)S(1)}, bf16[64,512]{0,1:T(8,128)(2,1)S(1)}, u32[]{:S(2)}, u32[]{:S(2)}) collective-permute-start(bf16[64,512]{0,1:T(8,128)(2,1)S(1)} %collective-permute-done.5), channel_id=1, source_target_pairs={{0,32},{32,64},{64,96},{96,128},{128,160},{160,192},{192,224},{224... | collective-permute-start | bytes 196616 | tf_op jit(solution)/shard_map/ppermute | solution.py:74
  46.1 37.6 %all-to-all-start = ((bf16[32,144,64]{1,2,0:T(8,128)(2,1)}), bf16[32,144,64]{1,2,0:T(8,128)(2,1)}, u32[]{:S(2)}, u32[]{:S(2)}) async-start(bf16[32,144,64]{1,2,0:T(8,128)(2,1)} %broadcast_in_dim.19), calls=%async_computation | async-start | bytes 2097152 | tf_op jit(solution)/shard_map/all_to_all | solution.py:15
  59.6 71.1 %all-gather.5.cloned.1.call-start = ((), (), s32[]{:S(2)}) async-start(), calls=%async_computation.4 | async-start | bytes 5013504 | tf_op jit(solution)/shard_map/all_gather | solution.py:32
  59.6 5.5 %collective-permute-start.14 = (bf16[64,512]{0,1:T(8,128)(2,1)S(1)}, bf16[64,512]{0,1:T(8,128)(2,1)S(1)}, u32[]{:S(2)}, u32[]{:S(2)}) collective-permute-start(bf16[64,512]{0,1:T(8,128)(2,1)S(1)} %collective-permute-done.13), channel_id=1, source_target_pairs={{0,480},{32,0},{64,32},{96,64},{128,96},{160,128},{192,160},{224,1... | collective-permute-start | bytes 196616 | tf_op jit(solution)/shard_map/ppermute | solution.py:76
  62.0 5.6 %collective-permute-start.7 = (bf16[64,512]{0,1:T(8,128)(2,1)S(1)}, bf16[64,512]{0,1:T(8,128)(2,1)S(1)}, u32[]{:S(2)}, u32[]{:S(2)}) collective-permute-start(bf16[64,512]{0,1:T(8,128)(2,1)S(1)} %collective-permute-done.6), channel_id=1, source_target_pairs={{0,32},{32,64},{64,96},{96,128},{128,160},{160,192},{192,224},{224... | collective-permute-start | bytes 196616 | tf_op jit(solution)/shard_map/ppermute | solution.py:74
  139.7 60.2 %all-to-all-start.1 = ((f32[32,144,64]{1,2,0:T(8,128)}), f32[32,144,64]{1,2,0:T(8,128)S(1)}, u32[]{:S(2)}, u32[]{:S(2)}) async-start(f32[32,144,64]{1,2,0:T(8,128)} %copy.38), calls=%async_computation.1 | async-start | bytes 4194304 | tf_op jit(solution)/shard_map/all_to_all | solution.py:43
  154.1 5.6 %collective-permute-start.15 = (bf16[64,512]{0,1:T(8,128)(2,1)S(1)}, bf16[64,512]{0,1:T(8,128)(2,1)S(1)}, u32[]{:S(2)}, u32[]{:S(2)}) collective-permute-start(bf16[64,512]{0,1:T(8,128)(2,1)S(1)} %select_bitcast_fusion), channel_id=1, source_target_pairs={{0,32},{32,64},{64,96},{96,128},{128,160},{160,192},{192,224},{224... | collective-permute-start | bytes 196616 | tf_op jit(solution)/shard_map/ppermute | solution.py:74
  154.1 5.6 %collective-permute-start.23 = (bf16[64,512]{0,1:T(8,128)(2,1)S(1)}, bf16[64,512]{0,1:T(8,128)(2,1)S(1)}, u32[]{:S(2)}, u32[]{:S(2)}) collective-permute-start(bf16[64,512]{0,1:T(8,128)(2,1)S(1)} %select_bitcast_fusion), channel_id=1, source_target_pairs={{0,480},{32,0},{64,32},{96,64},{128,96},{160,128},{192,160},{224,1... | collective-permute-start | bytes 196616 | tf_op jit(solution)/shard_map/ppermute | solution.py:76
  159.7 5.6 %collective-permute-start.16 = (bf16[64,512]{0,1:T(8,128)(2,1)S(1)}, bf16[64,512]{0,1:T(8,128)(2,1)S(1)}, u32[]{:S(2)}, u32[]{:S(2)}) collective-permute-start(bf16[64,512]{0,1:T(8,128)(2,1)S(1)} %collective-permute-done.15), channel_id=1, source_target_pairs={{0,32},{32,64},{64,96},{96,128},{128,160},{160,192},{192,224},{224... | collective-permute-start | bytes 196616 | tf_op jit(solution)/shard_map/ppermute | solution.py:74
  159.7 5.8 %collective-permute-start.24 = (bf16[64,512]{0,1:T(8,128)(2,1)S(1)}, bf16[64,512]{0,1:T(8,128)(2,1)S(1)}, u32[]{:S(2)}, u32[]{:S(2)}) collective-permute-start(bf16[64,512]{0,1:T(8,128)(2,1)S(1)} %collective-permute-done.23), channel_id=1, source_target_pairs={{0,480},{32,0},{64,32},{96,64},{128,96},{160,128},{192,160},{224,1... | collective-permute-start | bytes 196616 | tf_op jit(solution)/shard_map/ppermute | solution.py:76
  165.3 5.6 %collective-permute-start.17 = (bf16[64,512]{0,1:T(8,128)(2,1)S(1)}, bf16[64,512]{0,1:T(8,128)(2,1)S(1)}, u32[]{:S(2)}, u32[]{:S(2)}) collective-permute-start(bf16[64,512]{0,1:T(8,128)(2,1)S(1)} %collective-permute-done.16), channel_id=1, source_target_pairs={{0,32},{32,64},{64,96},{96,128},{128,160},{160,192},{192,224},{224... | collective-permute-start | bytes 196616 | tf_op jit(solution)/shard_map/ppermute | solution.py:74
  165.5 42.1 %collective-permute-start.25 = (bf16[64,512]{0,1:T(8,128)(2,1)S(1)}, bf16[64,512]{0,1:T(8,128)(2,1)S(1)}, u32[]{:S(2)}, u32[]{:S(2)}) collective-permute-start(bf16[64,512]{0,1:T(8,128)(2,1)S(1)} %collective-permute-done.24), channel_id=1, source_target_pairs={{0,480},{32,0},{64,32},{96,64},{128,96},{160,128},{192,160},{224,1... | collective-permute-start | bytes 196616 | tf_op jit(solution)/shard_map/ppermute | solution.py:76
  170.9 37.7 %collective-permute-start.18 = (bf16[64,512]{0,1:T(8,128)(2,1)S(1)}, bf16[64,512]{0,1:T(8,128)(2,1)S(1)}, u32[]{:S(2)}, u32[]{:S(2)}) collective-permute-start(bf16[64,512]{0,1:T(8,128)(2,1)S(1)} %collective-permute-done.17), channel_id=1, source_target_pairs={{0,32},{32,64},{64,96},{96,128},{128,160},{160,192},{192,224},{224... | collective-permute-start | bytes 196616 | tf_op jit(solution)/shard_map/ppermute | solution.py:74
  200.0 28.9 %copy-start.2 = (f32[144,64]{0,1:T(8,128)}, f32[144,64]{0,1:T(8,128)S(1)}, u32[]{:S(2)}) copy-start(f32[144,64]{0,1:T(8,128)S(1)} %reduce_sum.85) | copy-start | bytes 110596
  201.2 39.5 %all-to-all-start.2 = ((bf16[32,144,64]{1,2,0:T(8,128)(2,1)}), bf16[32,144,64]{1,2,0:T(8,128)(2,1)}, u32[]{:S(2)}, u32[]{:S(2)}) async-start(bf16[32,144,64]{1,2,0:T(8,128)(2,1)} %broadcast_in_dim.20), calls=%async_computation.2 | async-start | bytes 2097152 | tf_op jit(solution)/shard_map/all_to_all | solution.py:15
  207.5 80.5 %all-gather.7.cloned.1.call-start = ((), (), s32[]{:S(2)}) async-start(), calls=%async_computation.5 | async-start | bytes 5013504 | tf_op jit(solution)/shard_map/all_gather | solution.py:32
  207.6 3.5 collective-permute-start.26
  208.6 5.8 %collective-permute-start.19 = (bf16[64,512]{0,1:T(8,128)(2,1)S(1)}, bf16[64,512]{0,1:T(8,128)(2,1)S(1)}, u32[]{:S(2)}, u32[]{:S(2)}) collective-permute-start(bf16[64,512]{0,1:T(8,128)(2,1)S(1)} %collective-permute-done.18), channel_id=1, source_target_pairs={{0,32},{32,64},{64,96},{96,128},{128,160},{160,192},{192,224},{224... | collective-permute-start | bytes 196616 | tf_op jit(solution)/shard_map/ppermute | solution.py:74
  211.1 5.8 %collective-permute-start.27 = (bf16[64,512]{0,1:T(8,128)(2,1)S(1)}, bf16[64,512]{0,1:T(8,128)(2,1)S(1)}, u32[]{:S(2)}, u32[]{:S(2)}) collective-permute-start(bf16[64,512]{0,1:T(8,128)(2,1)S(1)} %collective-permute-done.26), channel_id=1, source_target_pairs={{0,480},{32,0},{64,32},{96,64},{128,96},{160,128},{192,160},{224,1... | collective-permute-start | bytes 196616 | tf_op jit(solution)/shard_map/ppermute | solution.py:76
  214.4 6.0 %collective-permute-start.20 = (bf16[64,512]{0,1:T(8,128)(2,1)S(1)}, bf16[64,512]{0,1:T(8,128)(2,1)S(1)}, u32[]{:S(2)}, u32[]{:S(2)}) collective-permute-start(bf16[64,512]{0,1:T(8,128)(2,1)S(1)} %collective-permute-done.19), channel_id=1, source_target_pairs={{0,32},{32,64},{64,96},{96,128},{128,160},{160,192},{192,224},{224... | collective-permute-start | bytes 196616 | tf_op jit(solution)/shard_map/ppermute | solution.py:74
  217.0 6.0 %collective-permute-start.28 = (bf16[64,512]{0,1:T(8,128)(2,1)S(1)}, bf16[64,512]{0,1:T(8,128)(2,1)S(1)}, u32[]{:S(2)}, u32[]{:S(2)}) collective-permute-start(bf16[64,512]{0,1:T(8,128)(2,1)S(1)} %collective-permute-done.27), channel_id=1, source_target_pairs={{0,480},{32,0},{64,32},{96,64},{128,96},{160,128},{192,160},{224,1... | collective-permute-start | bytes 196616 | tf_op jit(solution)/shard_map/ppermute | solution.py:76
  220.4 6.0 %collective-permute-start.21 = (bf16[64,512]{0,1:T(8,128)(2,1)S(1)}, bf16[64,512]{0,1:T(8,128)(2,1)S(1)}, u32[]{:S(2)}, u32[]{:S(2)}) collective-permute-start(bf16[64,512]{0,1:T(8,128)(2,1)S(1)} %collective-permute-done.20), channel_id=1, source_target_pairs={{0,32},{32,64},{64,96},{96,128},{128,160},{160,192},{192,224},{224... | collective-permute-start | bytes 196616 | tf_op jit(solution)/shard_map/ppermute | solution.py:74
  223.0 6.0 %collective-permute-start.29 = (bf16[64,512]{0,1:T(8,128)(2,1)S(1)}, bf16[64,512]{0,1:T(8,128)(2,1)S(1)}, u32[]{:S(2)}, u32[]{:S(2)}) collective-permute-start(bf16[64,512]{0,1:T(8,128)(2,1)S(1)} %collective-permute-done.28), channel_id=1, source_target_pairs={{0,480},{32,0},{64,32},{96,64},{128,96},{160,128},{192,160},{224,1... | collective-permute-start | bytes 196616 | tf_op jit(solution)/shard_map/ppermute | solution.py:76
  226.4 5.6 %collective-permute-start.22 = (bf16[64,512]{0,1:T(8,128)(2,1)S(1)}, bf16[64,512]{0,1:T(8,128)(2,1)S(1)}, u32[]{:S(2)}, u32[]{:S(2)}) collective-permute-start(bf16[64,512]{0,1:T(8,128)(2,1)S(1)} %collective-permute-done.21), channel_id=1, source_target_pairs={{0,32},{32,64},{64,96},{96,128},{128,160},{160,192},{192,224},{224... | collective-permute-start | bytes 196616 | tf_op jit(solution)/shard_map/ppermute | solution.py:74
  240.7 50.2 %copy-start.1 = (bf16[512,2048]{1,0:T(8,128)(2,1)}, bf16[512,2048]{1,0:T(8,128)(2,1)S(1)}, u32[]{:S(2)}) copy-start(bf16[512,2048]{1,0:T(8,128)(2,1)S(1)} %exponential_convert_fusion) | copy-start | bytes 6291460
  357.9 0.8 copy-start.3
  357.9 0.9 copy-start.5
Sparse Core Ops, SparseCore 0:
  86.6 44.0 all-gather.4
  244.4 43.5 all-gather.6
